TPU v7x, 32 devices: a whole 2x2x4 slice. The times are simulated.
32 devices in a mesh: inputs: 8 (over z, y), tm: 4 (over x, core).
Axes of the slice: x: 2, y: 2, z: 4, core: 2. Of those that a mesh axis runs over, the one named last changes fastest.
Arguments:
- voltages: bfloat16 [128, 131072], P('inputs', 'tm'), may hold values from -8 to 8
- pfb_taps: float32 [8, 512], replicated, may hold values from -2 to 2
Outputs:
- visibilities: float32 [256, 1, 2, 128, 128], P(('inputs', 'tm'))
All inputs are finite; a program needn't handle non-finite values.
Results may differ from a plain program's by a relative error of at most 0.002.
Values may be sent and summed in bfloat16 or wider, within the bound.
No kernel may reach another device: no remote copies, remote signals or barrier semaphores. Data moves between devices by JAX's collectives and lax.ppermute only.
A program may use at most 128 MiB of HBM per device.

v0:
```python
import jax
import jax.numpy as jnp
from jax import lax
from jax.sharding import PartitionSpec as P

F = 256
TAPS = 8
TILE = 128
FRAME = 512


def from_behind(value, axis, steps):
    count = lax.axis_size(axis)
    initial, last = (max(0, -steps), min(count, count - steps))
    return lax.ppermute(value, axis, [(source, source + steps) for source in range(initial, last)])


def dft_table(chans, length):
    rows = jnp.arange(2 * chans, dtype=jnp.int32)
    freq = rows // 2
    part = rows % 2
    samp = jnp.arange(length, dtype=jnp.int32)
    phase = freq[:, None] * samp[None, :] % length
    angle = 2.0 * jnp.pi / length * phase.astype(jnp.float32)
    vals = jnp.where(part[:, None] == 0, jnp.cos(angle), -jnp.sin(angle))
    return (vals * (1.0 / length**0.5)).astype(jnp.bfloat16)


def tile_sums(spec, scale):
    left = jnp.concatenate([spec[:, 0], spec[:, 1]], axis=-1)
    twisted = jnp.concatenate([spec[:, 1], -spec[:, 0]], axis=-1)
    count_in = left.shape[1]
    blocks = count_in // TILE
    chans = left.shape[0]
    real_rows = []
    imag_rows = []
    for first in range(blocks):
        lower = first * TILE
        cols = left[:, lower:]
        real_part = jnp.einsum(
            "cik,cjk->cij", left[:, lower : lower + TILE], cols, preferred_element_type=jnp.float32
        )
        imag_part = jnp.einsum(
            "cik,cjk->cij",
            twisted[:, lower : lower + TILE],
            cols,
            preferred_element_type=jnp.float32,
        )
        count = blocks - first
        real_rows.append(real_part.reshape(chans, TILE, count, TILE).transpose(0, 2, 1, 3))
        imag_rows.append(imag_part.reshape(chans, TILE, count, TILE).transpose(0, 2, 1, 3))
    real_all = jnp.concatenate(real_rows, axis=1)
    imag_all = jnp.concatenate(imag_rows, axis=1)
    return jnp.stack([real_all, imag_all], axis=2) * scale


def on_device(voltages, pfb_taps):
    inp_local = voltages.shape[0]
    frames_local = voltages.shape[1] // FRAME
    previous = from_behind(voltages[:, voltages.shape[1] - (TAPS - 1) * FRAME :], "tm", 1)
    extended = jnp.concatenate([previous, voltages], axis=1).reshape(
        inp_local, frames_local + TAPS - 1, FRAME
    )
    filtered = jnp.zeros((inp_local, frames_local, FRAME), jnp.float32)
    for tap in range(TAPS):
        filtered = filtered + pfb_taps[tap][None, None, :] * extended[
            :, tap : tap + frames_local, :
        ].astype(jnp.float32)
    filtered = filtered.astype(jnp.bfloat16)
    table = dft_table(F, FRAME)
    spectra = jnp.einsum("kn,itn->kit", table, filtered, preferred_element_type=jnp.float32)
    spectra = spectra.astype(jnp.bfloat16).reshape(F, 2, inp_local, frames_local)
    blocks_time = lax.axis_size("tm")
    scale = 1.0 / (frames_local * blocks_time)
    turned = lax.all_to_all(
        lax.all_to_all(spectra, "inputs", split_axis=0, concat_axis=2, tiled=True),
        "tm",
        split_axis=0,
        concat_axis=3,
        tiled=True,
    )
    return tile_sums(turned, scale)


def solution(mesh):
    in_specs = (P("inputs", "tm"), P())
    out_specs = P(("inputs", "tm"), None, None, None, None)
    return jax.shard_map(
        on_device, mesh=mesh, in_specs=in_specs, out_specs=out_specs, check_vma=False
    )
```

profile of v0, /device:TPU:0, one launch (start us, length us, event | category | flops | bytes accessed | tf_op | source)
XLA Modules:
  0.0 76.3 jit_solution(17021184768935166234)
XLA Ops:
  0.0 0.9 %slice.60 = bf16[16,3584]{1,0:T(8,128)(2,1)S(1)} slice(bf16[16,32768]{1,0:T(8,128)(2,1)} %param.2), slice={[0:16], [29184:32768]} | slice | bytes 229376 | tf_op jit(solution)/shard_map/slice | solution.py:60
  0.9 2.4 %collective-permute-start = (bf16[16,3584]{1,0:T(8,128)(2,1)S(1)}, bf16[16,3584]{1,0:T(8,128)(2,1)S(1)}, u32[]{:S(2)}, u32[]{:S(2)}) collective-permute-start(bf16[16,3584]{1,0:T(8,128)(2,1)S(1)} %slice.60), channel_id=1, source_target_pairs={{0,1},{1,2},{2,3},{4,5},{5,6},{6,7},{8,9},{9,10},{10,11},{12,13},{... | collective-permute-start | bytes 344072 | tf_op jit(solution)/shard_map/ppermute | solution.py:15
  3.3 1.0 %fusion.32 = (f32[1,512]{1,0:T(1,128)S(1)}, f32[1,512]{1,0:T(1,128)S(1)}, f32[1,512]{1,0:T(1,128)S(1)}, f32[1,512]{1,0:T(1,128)S(1)}, f32[1,512]{1,0:T(1,128)S(1...) fusion(f32[8,512]{1,0:T(8,128)} %param.3), kind=kLoop, calls=%fused_computation.48 | loop fusion | bytes 32768 | tf_op jit(solution)/shard_map/slice | solution.py:66
  4.4 0.0 collective-permute-done
  4.4 1.3 %pad_maximum_fusion = bf16[16,36352]{1,0:T(8,128)(2,1)S(1)} fusion(bf16[16,32768]{1,0:T(8,128)(2,1)} %param.2, bf16[16,3584]{1,0:T(8,128)(2,1)S(1)} %collective-permute-done), kind=kLoop, calls=%fused_computation.7 | loop fusion | flops 2326528 | bytes 2326528 | tf_op jit(solution)/shard_map/concatenate | solution.py:61
  5.7 0.7 reshape.74
  6.4 6.5 %convolution_convert_fusion = bf16[512,16,64]{0,2,1:T(8,128)(2,1)S(1)} fusion(bf16[16,71,512]{2,1,0:T(8,128)(2,1)S(1)} %reshape.74, f32[512]{0:T(512)S(1)} %bitcast.42, f32[512]{0:T(512)S(1)} %bitcast.43, f32[512]{0:T(512)S(1)} %bitcast.37, f32[512]{0:T(512)S(1)} %bitcast.38, f32[512]{0:T(512)S(1)} %bitcast.39, f32[512]{0:T(512)S(1)} %bitcast.40, ...), kind=kOutput, calls=%fused_computation.4 | convolution fusion | flops 554696704 | bytes 9456128 | tf_op jit(solution)/shard_map/kn,itn->kit/dot_general | solution.py:71
  12.9 2.0 %copy.11 = bf16[512,16,64]{2,1,0:T(8,128)(2,1)S(1)} copy(bf16[512,16,64]{0,2,1:T(8,128)(2,1)S(1)} %convolution_convert_fusion) | data formatting | bytes 2097152 | tf_op jit(solution)/shard_map/convert_element_type | solution.py:72
  15.0 1.7 %reshape.77 = bf16[8,2,32768]{2,1,0:T(2,128)(2,1)S(1)} reshape(bf16[256,2,16,64]{3,2,1,0:T(8,128)(2,1)S(1)} %bitcast.27) | data formatting | bytes 2097152
  16.7 32.5 %all_to_all.36 = bf16[8,2,32768]{2,1,0:T(2,128)(2,1)} all-to-all(bf16[8,2,32768]{2,1,0:T(2,128)(2,1)S(1)} %reshape.77), channel_id=1, replica_groups=mesh['inputs'=8,'tm'=4] {'inputs'}, dimensions={0} | all-to-all | bytes 2097152 | tf_op jit(solution)/shard_map/all_to_all | solution.py:76
  49.1 3.1 %reshape.78 = bf16[256,2,16,64]{3,2,1,0:T(8,128)(2,1)S(1)} reshape(bf16[8,2,32768]{2,1,0:T(2,128)(2,1)} %all_to_all.36) | data formatting | bytes 2097152
  52.2 2.0 %copy.12 = bf16[8,32,2,16,64]{4,3,0,2,1:T(8,128)(2,1)} copy(bf16[8,32,2,16,64]{4,3,2,1,0:T(8,128)(2,1)S(1)} %bitcast.28) | data formatting | bytes 2097152 | tf_op jit(solution)/shard_map/all_to_all | solution.py:76
  54.2 2.0 %copy.13 = bf16[32,2,128,64]{2,3,1,0:T(8,128)(2,1)S(1)} copy(bf16[32,2,128,64]{3,2,1,0:T(8,128)(2,1)} %bitcast.29) | data formatting | bytes 2097152 | tf_op jit(solution)/shard_map/all_to_all | solution.py:76
  56.2 17.4 %all_to_all.37 = bf16[32,2,128,64]{2,3,1,0:T(8,128)(2,1)S(1)} all-to-all(bf16[32,2,128,64]{2,3,1,0:T(8,128)(2,1)S(1)} %copy.13), channel_id=1, replica_groups=mesh['inputs'=8,'tm'=4] {'tm'}, dimensions={0} | all-to-all | bytes 2097152 | tf_op jit(solution)/shard_map/all_to_all | solution.py:75
  73.6 0.1 copy.14
  73.7 0.1 fusion.31
  73.8 0.2 copy.19
  74.0 0.2 copy.18
  74.3 0.4 convolution_bitcast_fusion.1
  74.7 0.4 convolution_bitcast_fusion
  75.2 0.1 maximum_multiply_fusion
  75.3 1.1 %copy.17 = f32[8,1,2,128,128]{4,3,2,1,0:T(8,128)} copy(f32[8,1,2,128,128]{4,3,0,2,1:T(8,128)S(1)} %maximum_multiply_fusion) | data formatting | bytes 2097152 | tf_op jit(solution)/shard_map/mul | solution.py:54
  (3 shorter events, 0.0 us)
Async XLA Ops:
  0.9 3.5 %collective-permute-start = (bf16[16,3584]{1,0:T(8,128)(2,1)S(1)}, bf16[16,3584]{1,0:T(8,128)(2,1)S(1)}, u32[]{:S(2)}, u32[]{:S(2)}) collective-permute-start(bf16[16,3584]{1,0:T(8,128)(2,1)S(1)} %slice.60), channel_id=1, source_target_pairs={{0,1},{1,2},{2,3},{4,5},{5,6},{6,7},{8,9},{9,10},{10,11},{12,13},{... | collective-permute-start | bytes 344072 | tf_op jit(solution)/shard_map/ppermute | solution.py:15
where the time goes:
time: 76.7 us; the launch traced here: 76.3 us
  blocking collectives  49.9 us (65%)
  local copies, waits for them, and re-layouts  15.1 us (20%)
  matrix products  7.4 us (10%)
  starting transfers between devices  2.39 us (3%)
  other arithmetic  1.43 us (2%)
    all_to_all x1, blocking collectives, on_device(): lax.all_to_all(spectra, 'inputs', split_axis=0, concat_axis=2, tiled=True)  32.5 us
    all_to_all x1, blocking collectives, on_device(): lax.all_to_all(lax.all_to_all(spectra, 'inputs', split_axis=0, concat_axi...  17.4 us
    dot_general x1, matrix products, on_device(): jnp.einsum('kn,itn->kit', table, filtered, preferred_element_type=jnp.flo...  6.55 us
    unnamed x4, local copies, waits for them, and re-layouts  5.2 us
    all_to_all x2, local copies, waits for them, and re-layouts, on_device(): lax.all_to_all(spectra, 'inputs', split_axis=0, concat_axis=2, tiled=True)  3.96 us
    ppermute x1, starting transfers between devices, from_behind(): lax.ppermute(value, axis, [(source, source + steps) for source in range(i...  2.39 us
    convert_element_type x1, local copies, waits for them, and re-layouts, on_device(): spectra.astype(jnp.bfloat16).reshape(F, 2, inp_local, frames_local)  2.03 us
  transfers between devices with their start and end apart: 1, of which 0 were waited for; matrix products, arithmetic and copies ran while one was open for 1% of the time, Pallas kernels for 0%

commit v1 on v0

--- a/solution.py
+++ b/solution.py
@@ -7,6 +7,18 @@
 TAPS = 8
 TILE = 128
 FRAME = 512
+
+
+def trails_balance(row_data):
+    return jnp.concatenate(
+        lax.all_to_all(
+            jnp.stack(jnp.split(row_data, lax.axis_size("inputs"), 0)),
+            "inputs",
+            split_axis=0,
+            concat_axis=0,
+        ),
+        2,
+    )
 
 
 def from_behind(value, axis, steps):
@@ -72,13 +84,7 @@
     spectra = spectra.astype(jnp.bfloat16).reshape(F, 2, inp_local, frames_local)
     blocks_time = lax.axis_size("tm")
     scale = 1.0 / (frames_local * blocks_time)
-    turned = lax.all_to_all(
-        lax.all_to_all(spectra, "inputs", split_axis=0, concat_axis=2, tiled=True),
-        "tm",
-        split_axis=0,
-        concat_axis=3,
-        tiled=True,
-    )
+    turned = lax.all_to_all(trails_balance(spectra), "tm", split_axis=0, concat_axis=3, tiled=True)
     return tile_sums(turned, scale)
 
 

time: 76.7 us -> 83.9 us (1.094)
  local copies, waits for them, and re-layouts: 15.1 us -> 22.2 us
    split x0 -> x9, local copies, waits for them, and re-layouts: none -> 6.7 us  [trails_balance(): jnp.split(row_data, lax.axis_size('inputs'), 0)]
    reshape x0 -> x2, local copies, waits for them, and re-layouts: none -> 3.96 us  [trails_balance(): jnp.concatenate(lax.all_to_all(jnp.stack(jnp.split(row_data, lax.axis_siz...]
    all_to_all x3 -> x1, local copies, waits for them, and re-layouts: 4.05 us -> 0.09 us  [on_device(): lax.all_to_all(trails_balance(spectra), 'tm', split_axis=0, concat_axis=3...]
    unnamed x4 -> x15, local copies, waits for them, and re-layouts: 5.2 us -> 7.57 us
    convert_element_type x1 -> x0, local copies, waits for them, and re-layouts: 2.03 us -> none  [on_device(): spectra.astype(jnp.bfloat16).reshape(F, 2, inp_local, frames_local)]
where the time goes in v1:
time: 83.9 us; the launch traced here: 83.4 us
  blocking collectives  49.8 us (59%)
  local copies, waits for them, and re-layouts  22.2 us (26%)
  matrix products  7.4 us (9%)
  starting transfers between devices  2.39 us (3%)
  other arithmetic  1.43 us (2%)
    all_to_all x1, blocking collectives, trails_balance(): lax.all_to_all(jnp.stack(jnp.split(row_data, lax.axis_size('inputs'), 0))...  32.4 us
    all_to_all x1, blocking collectives, on_device(): lax.all_to_all(trails_balance(spectra), 'tm', split_axis=0, concat_axis=3...  17.4 us
    unnamed x15, local copies, waits for them, and re-layouts  7.57 us
    split x9, local copies, waits for them, and re-layouts, trails_balance(): jnp.split(row_data, lax.axis_size('inputs'), 0)  6.7 us
    dot_general x1, matrix products, on_device(): jnp.einsum('kn,itn->kit', table, filtered, preferred_element_type=jnp.flo...  6.55 us
    reshape x2, local copies, waits for them, and re-layouts, trails_balance(): jnp.concatenate(lax.all_to_all(jnp.stack(jnp.split(row_data, lax.axis_siz...  3.96 us
    ppermute x1, starting transfers between devices, from_behind(): lax.ppermute(value, axis, [(source, source + steps) for source in range(i...  2.39 us
  transfers between devices with their start and end apart: 1, of which 0 were waited for; matrix products, arithmetic and copies ran while one was open for 1% of the time, Pallas kernels for 0%

profile of v1, /device:TPU:0, one launch (start us, length us, event | category | flops | bytes accessed | tf_op | source)
XLA Modules:
  0.0 83.4 jit_solution(18238531320039831594)
XLA Ops:
  0.0 0.9 %slice.68 = bf16[16,3584]{1,0:T(8,128)(2,1)S(1)} slice(bf16[16,32768]{1,0:T(8,128)(2,1)} %param.2), slice={[0:16], [29184:32768]} | slice | bytes 229376 | tf_op jit(solution)/shard_map/slice | solution.py:72
  0.9 2.4 %collective-permute-start = (bf16[16,3584]{1,0:T(8,128)(2,1)S(1)}, bf16[16,3584]{1,0:T(8,128)(2,1)S(1)}, u32[]{:S(2)}, u32[]{:S(2)}) collective-permute-start(bf16[16,3584]{1,0:T(8,128)(2,1)S(1)} %slice.68), channel_id=1, source_target_pairs={{0,1},{1,2},{2,3},{4,5},{5,6},{6,7},{8,9},{9,10},{10,11},{12,13},{... | collective-permute-start | bytes 344072 | tf_op jit(solution)/shard_map/ppermute | solution.py:27
  3.3 1.0 %fusion.33 = (f32[1,512]{1,0:T(1,128)S(1)}, f32[1,512]{1,0:T(1,128)S(1)}, f32[1,512]{1,0:T(1,128)S(1)}, f32[1,512]{1,0:T(1,128)S(1)}, f32[1,512]{1,0:T(1,128)S(1...) fusion(f32[8,512]{1,0:T(8,128)} %param.3), kind=kLoop, calls=%fused_computation.57 | loop fusion | bytes 32768 | tf_op jit(solution)/shard_map/slice | solution.py:78
  4.4 1.3 %pad_maximum_fusion = bf16[16,36352]{1,0:T(8,128)(2,1)S(1)} fusion(bf16[16,32768]{1,0:T(8,128)(2,1)} %param.2, bf16[16,3584]{1,0:T(8,128)(2,1)S(1)} %collective-permute-done), kind=kLoop, calls=%fused_computation.7 | loop fusion | flops 2326528 | bytes 2326528 | tf_op jit(solution)/shard_map/concatenate | solution.py:73
  5.7 0.7 reshape.94
  6.4 6.5 %convolution_convert_fusion = bf16[512,16,64]{0,2,1:T(8,128)(2,1)S(1)} fusion(bf16[16,71,512]{2,1,0:T(8,128)(2,1)S(1)} %reshape.94, f32[512]{0:T(512)S(1)} %bitcast.54, f32[512]{0:T(512)S(1)} %bitcast.55, f32[512]{0:T(512)S(1)} %bitcast.49, f32[512]{0:T(512)S(1)} %bitcast.50, f32[512]{0:T(512)S(1)} %bitcast.51, f32[512]{0:T(512)S(1)} %bitcast.52, ...), kind=kOutput, calls=%fused_computation.4 | convolution fusion | flops 554696704 | bytes 9456128 | tf_op jit(solution)/shard_map/kn,itn->kit/dot_general | solution.py:83
  12.9 0.6 fusion.32
  13.8 0.9 %copy.36 = bf16[64,16,64]{2,1,0:T(8,128)(2,1)} copy(bf16[64,16,64]{0,2,1:T(8,128)(2,1)S(1)} %get-tuple-element.8) | data formatting | bytes 262144 | tf_op jit(solution)/shard_map/split | solution.py:15
  14.7 0.9 %copy.35 = bf16[64,16,64]{2,1,0:T(8,128)(2,1)} copy(bf16[64,16,64]{0,2,1:T(8,128)(2,1)S(1)} %get-tuple-element.9) | data formatting | bytes 262144 | tf_op jit(solution)/shard_map/split | solution.py:15
  15.9 0.9 %copy.33 = bf16[64,16,64]{2,1,0:T(8,128)(2,1)} copy(bf16[64,16,64]{0,2,1:T(8,128)(2,1)S(1)} %get-tuple-element.11) | data formatting | bytes 262144 | tf_op jit(solution)/shard_map/split | solution.py:15
  16.9 0.9 %copy.32 = bf16[64,16,64]{2,1,0:T(8,128)(2,1)} copy(bf16[64,16,64]{0,2,1:T(8,128)(2,1)S(1)} %get-tuple-element.12) | data formatting | bytes 262144 | tf_op jit(solution)/shard_map/split | solution.py:15
  17.8 0.9 %copy.31 = bf16[64,16,64]{2,1,0:T(8,128)(2,1)} copy(bf16[64,16,64]{0,2,1:T(8,128)(2,1)S(1)} %get-tuple-element.13) | data formatting | bytes 262144 | tf_op jit(solution)/shard_map/split | solution.py:15
  18.7 0.9 %copy.30 = bf16[64,16,64]{2,1,0:T(8,128)(2,1)} copy(bf16[64,16,64]{0,2,1:T(8,128)(2,1)S(1)} %get-tuple-element.14) | data formatting | bytes 262144 | tf_op jit(solution)/shard_map/split | solution.py:15
  19.7 1.0 %constant_dynamic-update-slice_fusion.7 = bf16[8,32,2,16,64]{4,3,2,1,0:T(8,128)(2,1)S(1)} fusion(bf16[1,32,2,16,64]{4,3,2,1,0:T(8,128)(2,1)} %bitcast.45), kind=kLoop, calls=%fused_computation.35 | loop fusion | bytes 393216
  20.6 1.0 %constant_dynamic-update-slice_fusion.6 = bf16[8,32,2,16,64]{4,3,2,1,0:T(8,128)(2,1)S(1)} fusion(bf16[8,32,2,16,64]{4,3,2,1,0:T(8,128)(2,1)S(1)} %constant_dynamic-update-slice_fusion.7, bf16[1,32,2,16,64]{4,3,2,1,0:T(8,128)(2,1)} %bitcast.44), kind=kLoop, calls=%fused_computation.34 | loop fusion | bytes 393216
  21.6 1.0 %constant_dynamic-update-slice_fusion.5 = bf16[8,32,2,16,64]{4,3,2,1,0:T(8,128)(2,1)S(1)} fusion(bf16[8,32,2,16,64]{4,3,2,1,0:T(8,128)(2,1)S(1)} %constant_dynamic-update-slice_fusion.6, bf16[1,32,2,16,64]{4,3,2,1,0:T(8,128)(2,1)} %bitcast.43), kind=kLoop, calls=%fused_computation.33 | loop fusion | bytes 393216
  22.6 1.0 %constant_dynamic-update-slice_fusion.4 = bf16[8,32,2,16,64]{4,3,2,1,0:T(8,128)(2,1)S(1)} fusion(bf16[8,32,2,16,64]{4,3,2,1,0:T(8,128)(2,1)S(1)} %constant_dynamic-update-slice_fusion.5, bf16[1,32,2,16,64]{4,3,2,1,0:T(8,128)(2,1)} %bitcast.42), kind=kLoop, calls=%fused_computation.32 | loop fusion | bytes 393216
  23.8 1.7 %reshape.98 = bf16[8,2,32768]{2,1,0:T(2,128)(2,1)S(1)} reshape(bf16[8,32,2,16,64]{4,3,2,1,0:T(8,128)(2,1)S(1)} %constant_dynamic-update-slice_fusion) | data formatting | bytes 2097152
  25.5 32.4 %all_to_all.23 = bf16[8,2,32768]{2,1,0:T(2,128)(2,1)S(1)} all-to-all(bf16[8,2,32768]{2,1,0:T(2,128)(2,1)S(1)} %reshape.98), channel_id=1, replica_groups=mesh['inputs'=8,'tm'=4] {'inputs'}, dimensions={0} | all-to-all | bytes 2097152 | tf_op jit(solution)/shard_map/all_to_all | solution.py:14
  57.8 1.4 %reshape.99 = bf16[8,32,2,16,64]{4,3,2,1,0:T(8,128)(2,1)S(1)} reshape(bf16[8,2,32768]{2,1,0:T(2,128)(2,1)S(1)} %all_to_all.23) | data formatting | bytes 2097152
  59.3 2.0 %copy.38 = bf16[32,2,8,16,64]{4,3,2,1,0:T(8,128)(2,1)} copy(bf16[32,2,8,16,64]{4,3,1,0,2:T(8,128)(2,1)S(1)} %bitcast.32) | data formatting | bytes 2097152 | tf_op jit(solution)/shard_map/reshape | solution.py:13
  61.2 2.0 %copy.39 = bf16[32,2,128,64]{2,3,1,0:T(8,128)(2,1)S(1)} copy(bf16[32,2,128,64]{3,2,1,0:T(8,128)(2,1)} %bitcast.33) | data formatting | bytes 2097152 | tf_op jit(solution)/shard_map/reshape | solution.py:13
  63.2 17.4 %all_to_all.24 = bf16[32,2,128,64]{2,3,1,0:T(8,128)(2,1)S(1)} all-to-all(bf16[32,2,128,64]{2,3,1,0:T(8,128)(2,1)S(1)} %copy.39), channel_id=1, replica_groups=mesh['inputs'=8,'tm'=4] {'tm'}, dimensions={0} | all-to-all | bytes 2097152 | tf_op jit(solution)/shard_map/all_to_all | solution.py:87
  82.3 1.1 %copy.43 = f32[8,1,2,128,128]{4,3,2,1,0:T(8,128)} copy(f32[8,1,2,128,128]{4,3,0,2,1:T(8,128)S(1)} %maximum_multiply_fusion) | data formatting | bytes 2097152 | tf_op jit(solution)/shard_map/mul | solution.py:66
  (21 shorter events, 2.3 us)
Async XLA Ops:
  0.9 3.5 %collective-permute-start = (bf16[16,3584]{1,0:T(8,128)(2,1)S(1)}, bf16[16,3584]{1,0:T(8,128)(2,1)S(1)}, u32[]{:S(2)}, u32[]{:S(2)}) collective-permute-start(bf16[16,3584]{1,0:T(8,128)(2,1)S(1)} %slice.68), channel_id=1, source_target_pairs={{0,1},{1,2},{2,3},{4,5},{5,6},{6,7},{8,9},{9,10},{10,11},{12,13},{... | collective-permute-start | bytes 344072 | tf_op jit(solution)/shard_map/ppermute | solution.py:27
  16.9 6.8 %copy-start.1 = (bf16[64,16,64]{2,1,0:T(8,128)(2,1)S(1)}, bf16[64,16,64]{2,1,0:T(8,128)(2,1)}, u32[]{:S(2)}) copy-start(bf16[64,16,64]{2,1,0:T(8,128)(2,1)} %copy.35) | copy-start | bytes 393220
  17.8 5.9 %copy-start = (bf16[64,16,64]{2,1,0:T(8,128)(2,1)S(1)}, bf16[64,16,64]{2,1,0:T(8,128)(2,1)}, u32[]{:S(2)}) copy-start(bf16[64,16,64]{2,1,0:T(8,128)(2,1)} %copy.36) | copy-start | bytes 393220
